TPU v7x, 512 devices: a whole 4x4x16 slice. The times are simulated.
512 devices in a mesh: dp: 8 (over y, core), expert: 64 (over x, z).
Axes of the slice: x: 4, y: 4, z: 16, core: 2. Of those that a mesh axis runs over, the one named last changes fastest.
Arguments:
- tokens: bfloat16 [4096, 2048], P('expert', 'dp'), may hold values from -6 to 6
- expert_ids: int32 [4096, 8], P('expert'), may hold values from 0 to 127, all different within a row; in each aligned block of 64 rows (0 to 63, 64 to 127, ...) at most 6 rows name the same one
- route_weights: bfloat16 [4096, 8], P('expert'), may hold values from 0.019897461 to 0.3984375
- w_gate: bfloat16 [128, 2048, 1024], P('expert', None, 'dp'), may hold values from -0.125 to 0.125
- w_up: bfloat16 [128, 2048, 1024], P('expert', None, 'dp'), may hold values from -0.125 to 0.125
- w_down: bfloat16 [128, 1024, 2048], P('expert', 'dp'), may hold values from -0.1875 to 0.1875
Outputs:
- moe_out: bfloat16 [4096, 2048], P('expert', 'dp')
Inputs may be any that keep to these rules, and one draw needn't show every extreme that they name: `expert_ids`: each token names 8 different experts. In each aligned block of 64 rows no expert is named more than 6 times, a bound that some block reaches.
All inputs are finite; a program needn't handle non-finite values.
Results may differ from a plain program's by a relative error of at most 0.019.
Values may be sent and summed in bfloat16 or wider, within the bound.
A program may use at most 64 MiB of HBM per device.

v0:
```python
import jax
import jax.numpy as jnp
from jax import lax
from jax.sharding import PartitionSpec as P


def slot_tables(expert_ids, route_weights, expert_count, capacity):
    flat_ids = expert_ids.reshape(-1)
    expert_range = jnp.arange(expert_count, dtype=jnp.int32)
    one_hot = (flat_ids[:, None] == expert_range[None, :]).astype(jnp.int32)
    ranks = jnp.sum((jnp.cumsum(one_hot, axis=0) - 1) * one_hot, axis=1)
    dest_slot = (flat_ids * capacity + ranks).reshape(expert_ids.shape)
    slot_range = jnp.arange(expert_count * capacity, dtype=jnp.int32)
    hit_table = dest_slot[None, :, :] == slot_range[:, None, None]
    dispatch_matrix = jnp.sum(hit_table.astype(jnp.float32), axis=2).astype(jnp.bfloat16)
    weight_table = jnp.where(
        hit_table, route_weights.astype(jnp.float32)[None, :, :], jnp.float32(0.0)
    )
    combine_matrix = jnp.sum(weight_table, axis=2).astype(jnp.bfloat16)
    return (dispatch_matrix, combine_matrix)


def finish_expert(gate_proj, up_proj, w_down):
    hidden = (jax.nn.silu(gate_proj) * up_proj).astype(jnp.bfloat16)
    return jnp.einsum("nrcf,rfd->nrcd", hidden, w_down, preferred_element_type=jnp.float32).astype(
        jnp.bfloat16
    )


def on_device(tokens, expert_ids, route_weights, w_gate, w_up, w_down):
    peer_count = lax.axis_size("expert")
    local_experts = w_gate.shape[0]
    expert_count = local_experts * peer_count
    tok_rows, top_count = expert_ids.shape
    capacity = tok_rows * top_count * 3 // (2 * expert_count)
    dispatch_matrix, combine_matrix = slot_tables(expert_ids, route_weights, expert_count, capacity)
    whole = lax.all_gather(tokens, "dp", axis=1, tiled=True)
    send_rows = jnp.dot(dispatch_matrix, whole, preferred_element_type=jnp.float32).astype(
        jnp.bfloat16
    )
    send_rows = send_rows.reshape(peer_count, local_experts, capacity, whole.shape[1])
    arrived = lax.all_to_all(send_rows, "expert", split_axis=0, concat_axis=0, tiled=True)
    gate_proj = jnp.einsum("nrcd,rdf->nrcf", arrived, w_gate, preferred_element_type=jnp.float32)
    up_proj = jnp.einsum("nrcd,rdf->nrcf", arrived, w_up, preferred_element_type=jnp.float32)
    expert_rows = finish_expert(gate_proj, up_proj, w_down)
    returned = lax.all_to_all(expert_rows, "expert", split_axis=0, concat_axis=0, tiled=True)
    flat_returned = returned.reshape(expert_count * capacity, returned.shape[3])
    mixed_rows = lax.dot_general(
        combine_matrix, flat_returned, (((0,), (0,)), ((), ())), preferred_element_type=jnp.float32
    )
    return lax.psum_scatter(mixed_rows.astype(jnp.bfloat16), "dp", scatter_dimension=1, tiled=True)


def solution(mesh):
    return jax.shard_map(
        on_device,
        mesh=mesh,
        in_specs=(
            P("expert", "dp"),
            P("expert", None),
            P("expert", None),
            P("expert", None, "dp"),
            P("expert", None, "dp"),
            P("expert", "dp", None),
        ),
        out_specs=P("expert", "dp"),
        check_vma=False,
    )
```

profile of v0, /device:TPU:1, one launch (start us, length us, event | category | flops | bytes accessed | tf_op | source)
XLA Modules:
  0.0 416.7 jit_solution(11392005861760912767)
XLA Ops:
  6.5 0.0 copy-start
  6.5 0.0 reduce-scatter.2.cloned.1.call-start
  6.5 0.9 copy.53
  7.4 0.1 eq.42
  7.5 0.1 eq.38
  7.6 0.8 copy.59
  8.3 0.1 copy.55
  8.5 0.2 fusion.29
  8.7 0.1 add_add_fusion
  8.8 0.2 fusion.28
  9.0 0.1 reduce_sum.30
  9.1 0.1 copy.57
  9.2 0.7 multiply_add_fusion
  9.9 0.1 copy.58
  10.0 19.7 %all_gather.3 = bf16[64,2048]{1,0:T(8,128)(2,1)S(1)} all-gather(bf16[64,256]{1,0:T(8,128)(2,1)} %param.6), channel_id=1, replica_groups=mesh['dp'=8,'expert'=64] {'dp'}, dimensions={1}, use_global_device_ids=true | all-gather | bytes 294912 | tf_op jit(solution)/shard_map/all_gather | solution.py:37
  29.7 1.0 select_reduce_fusion
  30.8 2.7 convolution_convert_fusion
  33.4 6.3 %reshape.34 = bf16[64,2,6,2048]{3,2,1,0:T(8,128)(2,1)} reshape(bf16[768,2048]{1,0:T(8,128)(2,1)} %convolution_convert_fusion) | data formatting | bytes 6291456 | tf_op jit(solution)/shard_map/reshape | solution.py:41
  39.7 5.5 %copy.60 = bf16[64,2,6,2048]{3,1,2,0:T(2,128)(2,1)S(1)} copy(bf16[64,2,6,2048]{3,2,1,0:T(8,128)(2,1)} %reshape.34) | data formatting | bytes 6291456 | tf_op jit(solution)/shard_map/reshape | solution.py:41
  45.2 0.0 copy-start.2
  45.2 153.8 %all_to_all.10 = bf16[64,2,6,2048]{3,1,2,0:T(2,128)(2,1)S(1)} all-to-all(bf16[64,2,6,2048]{3,1,2,0:T(2,128)(2,1)S(1)} %copy.60), channel_id=1, replica_groups=mesh['dp'=8,'expert'=64] {'expert'}, dimensions={0} | all-to-all | bytes 6291456 | tf_op jit(solution)/shard_map/all_to_all | solution.py:42
  199.0 0.0 copy-start.1
  199.0 1.7 copy-done.1
  200.6 0.0 copy-done.2
  200.6 0.0 copy-start.3
  200.6 1.8 fusion.5
  202.5 0.0 copy-done
  202.5 0.0 copy-done.3
  202.5 6.3 %fusion = bf16[64,2,6,2048]{3,0,2,1:T(8,128)(2,1)} fusion(bf16[64,2,6,2048]{3,1,2,0:T(2,128)(2,1)} %copy-done.1, bf16[2,128,2048]{2,1,0:T(8,128)(2,1)S(1)} %copy-done, bf16[2,2048,128]{2,1,0:T(8,128)(2,1)S(1)} %copy-done.3, f32[64,2,6,128]{3,0,2,1:T(8,128)S(1)} %fusion.5), kind=kOutput, calls=%fused_computation.2 | convolution fusion | flops 807469056 | bytes 8781824 | tf_op jit(solution)/shard_map/nrcf,rfd->nrcd/dot_general | solution.py:25
  208.8 5.2 %copy.63 = bf16[64,2,6,2048]{3,1,2,0:T(2,128)(2,1)S(1)} copy(bf16[64,2,6,2048]{3,0,2,1:T(8,128)(2,1)} %fusion) | data formatting | bytes 6291456 | tf_op jit(solution)/shard_map/convert_element_type | solution.py:25
  214.0 150.3 %all_to_all.11 = bf16[64,2,6,2048]{3,1,2,0:T(2,128)(2,1)S(1)} all-to-all(bf16[64,2,6,2048]{3,1,2,0:T(2,128)(2,1)S(1)} %copy.63), channel_id=1, replica_groups=mesh['dp'=8,'expert'=64] {'expert'}, dimensions={0} | all-to-all | bytes 6291456 | tf_op jit(solution)/shard_map/all_to_all | solution.py:46
  364.2 3.6 copy.64
  367.8 6.3 %reshape.35 = bf16[768,2048]{1,0:T(8,128)(2,1)} reshape(bf16[64,2,6,2048]{3,2,1,0:T(8,128)(2,1)} %copy.64) | data formatting | bytes 6291456 | tf_op jit(solution)/shard_map/reshape | solution.py:47
  374.1 3.2 convolution_convert_fusion.2
  377.4 0.0 reduce-scatter.2.cloned.1.call-update
  377.4 32.4 %reduce-scatter.2.cloned.1.call-done = bf16[64,256]{1,0:T(8,128)(2,1)} async-done(((bf16[64,2048]{1,0:T(8,128)(2,1)}), bf16[64,256]{1,0:T(8,128)(2,1)}) %reduce-scatter.2.cloned.1.call-update) | async-done | bytes 32784 | tf_op jit(solution)/shard_map/reduce_scatter | solution.py:51
  (4 shorter events, 0.1 us)
Async XLA Ops:
  6.5 196.0 %copy-start = (bf16[2,128,2048]{2,1,0:T(8,128)(2,1)S(1)}, bf16[2,128,2048]{2,1,0:T(8,128)(2,1)}, u32[]{:S(2)}) copy-start(bf16[2,128,2048]{2,1,0:T(8,128)(2,1)} %param.11) | copy-start | bytes 3145732
  6.5 403.3 %reduce-scatter.2.cloned.1.call-start = ((), (), s32[]{:S(2)}) async-start(), calls=%async_computation.3 | async-start | bytes 294912 | tf_op jit(solution)/shard_map/reduce_scatter | solution.py:51
  45.2 155.5 %copy-start.2 = (bf16[2,2048,128]{2,1,0:T(8,128)(2,1)S(1)}, bf16[2,2048,128]{2,1,0:T(8,128)(2,1)}, u32[]{:S(2)}) copy-start(bf16[2,2048,128]{2,1,0:T(8,128)(2,1)} %param.9) | copy-start | bytes 3145732
  199.0 1.7 copy-start.1
  200.6 1.8 copy-start.3
Sparse Core Ops, SparseCore 0:
  377.5 32.2 reduce-scatter.1
where the time goes:
time: 418 us; the launch traced here: 417 us
  blocking collectives  324 us (78%)
  waiting for transfers between devices  32.5 us (8%)
  local copies, waits for them, and re-layouts  30.6 us (7%)
  matrix products  14.1 us (3%)
  between operations  13.5 us (3%)
    all_to_all x1, blocking collectives, on_device(): lax.all_to_all(send_rows, 'expert', split_axis=0, concat_axis=0, tiled=True)  154 us
    all_to_all x1, blocking collectives, on_device(): lax.all_to_all(expert_rows, 'expert', split_axis=0, concat_axis=0, tiled=...  150 us
    reduce_scatter x1, waiting for transfers between devices, on_device(): lax.psum_scatter(mixed_rows.astype(jnp.bfloat16), 'dp', scatter_dimension...  32.4 us
    all_gather x1, blocking collectives, on_device(): whole = lax.all_gather(tokens, 'dp', axis=1, tiled=True)  19.7 us
    reshape x2, local copies, waits for them, and re-layouts, on_device(): send_rows.reshape(peer_count, local_experts, capacity, whole.shape[1])  11.7 us
  transfers between devices with their start and end apart: 1, of which 1 were waited for; matrix products, arithmetic and copies ran while one was open for 0% of the time, Pallas kernels for 0%

commit v1 on v0

v1 whole, which is shorter than its diff:
```python
import jax
import jax.numpy as jnp
from jax import lax
from jax.sharding import PartitionSpec as P


def slot_tables(expert_ids, route_weights, expert_count, capacity):
    flat_ids = expert_ids.reshape(-1)
    expert_range = jnp.arange(expert_count, dtype=jnp.int32)
    one_hot = (flat_ids[:, None] == expert_range[None, :]).astype(jnp.int32)
    ranks = jnp.sum((jnp.cumsum(one_hot, axis=0) - 1) * one_hot, axis=1)
    dest_slot = (flat_ids * capacity + ranks).reshape(expert_ids.shape)
    slot_range = jnp.arange(expert_count * capacity, dtype=jnp.int32)
    hit_table = dest_slot[None, :, :] == slot_range[:, None, None]
    dispatch_matrix = jnp.sum(hit_table.astype(jnp.float32), axis=2).astype(jnp.bfloat16)
    weight_table = jnp.where(
        hit_table, route_weights.astype(jnp.float32)[None, :, :], jnp.float32(0.0)
    )
    combine_matrix = jnp.sum(weight_table, axis=2).astype(jnp.bfloat16)
    return (dispatch_matrix, combine_matrix)


def on_device(tokens, expert_ids, route_weights, w_gate, w_up, w_down):
    peer_count = lax.axis_size("expert")
    dp_count = lax.axis_size("dp")
    local_experts, width, group = w_gate.shape
    expert_count = local_experts * peer_count
    tok_rows, top_count = expert_ids.shape
    feats = tokens.shape[1]
    capacity = tok_rows * top_count * 3 // (2 * expert_count)
    dispatch_matrix, combine_matrix = slot_tables(expert_ids, route_weights, expert_count, capacity)
    send_rows = jnp.dot(dispatch_matrix, tokens, preferred_element_type=jnp.float32).astype(
        jnp.bfloat16
    )
    send_rows = send_rows.reshape(peer_count, local_experts * capacity, feats)
    arrived = lax.all_to_all(send_rows, "expert", split_axis=0, concat_axis=0, tiled=True)
    arrived = arrived.reshape(peer_count, local_experts, capacity, feats).transpose(1, 0, 2, 3)
    arrived = arrived.reshape(local_experts, peer_count * capacity, feats)
    whole = lax.all_gather(arrived, "dp", axis=0)
    w_gate = w_gate.reshape(local_experts, dp_count, feats, group)
    w_up = w_up.reshape(local_experts, dp_count, feats, group)
    gate_proj = jnp.einsum("grnd,rgdf->rnf", whole, w_gate, preferred_element_type=jnp.float32)
    up_proj = jnp.einsum("grnd,rgdf->rnf", whole, w_up, preferred_element_type=jnp.float32)
    hidden = (jax.nn.silu(gate_proj) * up_proj).astype(jnp.bfloat16)
    partial = jnp.einsum("rnf,rfd->rnd", hidden, w_down, preferred_element_type=jnp.float32)
    partial = partial.astype(jnp.bfloat16).reshape(local_experts * peer_count * capacity, width)
    summed = lax.psum_scatter(partial, "dp", scatter_dimension=1, tiled=True)
    summed = summed.reshape(local_experts, peer_count, capacity, feats).transpose(1, 0, 2, 3)
    summed = summed.reshape(peer_count, local_experts * capacity, feats)
    returned = lax.all_to_all(summed, "expert", split_axis=0, concat_axis=0, tiled=True)
    flat_returned = returned.reshape(expert_count * capacity, feats)
    return lax.dot_general(
        combine_matrix, flat_returned, (((0,), (0,)), ((), ())), preferred_element_type=jnp.float32
    ).astype(jnp.bfloat16)


def solution(mesh):
    return jax.shard_map(
        on_device,
        mesh=mesh,
        in_specs=(
            P("expert", "dp"),
            P("expert", None),
            P("expert", None),
            P("expert", None, "dp"),
            P("expert", None, "dp"),
            P("expert", "dp", None),
        ),
        out_specs=P("expert", "dp"),
        check_vma=False,
    )
```

time: 418 us -> 199 us (0.48)
  the two profiles are of different devices: /device:TPU:1 before, /device:TPU:31 now
where the time goes in v1:
time: 199 us
  blocking collectives  94.3 us (47%)
  waiting for transfers between devices  72.8 us (37%)
  between operations  13.5 us (7%)
  matrix products  10.1 us (5%)
  local copies, waits for them, and re-layouts  5.12 us (3%)
  other arithmetic  2.86 us (1%)
    all_to_all x1, blocking collectives, on_device(): lax.all_to_all(send_rows, 'expert', split_axis=0, concat_axis=0, tiled=True)  47.3 us
    all_to_all x1, blocking collectives, on_device(): lax.all_to_all(summed, 'expert', split_axis=0, concat_axis=0, tiled=True)  47.1 us
    reduce_scatter x1, waiting for transfers between devices, on_device(): summed = lax.psum_scatter(partial, 'dp', scatter_dimension=1, tiled=True)  42.7 us
    all_gather x1, waiting for transfers between devices, on_device(): whole = lax.all_gather(arrived, 'dp', axis=0)  30.1 us
    dot_general x1, matrix products, on_device(): jnp.einsum('rnf,rfd->rnd', hidden, w_down, preferred_element_type=jnp.flo...  5.44 us
  transfers between devices with their start and end apart: 2, of which 2 were waited for; matrix products, arithmetic and copies ran while one was open for 0% of the time, Pallas kernels for 0%

profile of v1, /device:TPU:31, one launch (start us, length us, event | category | flops | bytes accessed | tf_op | source)
XLA Modules:
  0.0 198.8 jit_solution(16926000078186183311)
XLA Ops:
  6.5 0.0 copy-start
  6.5 0.0 all-gather.2.cloned.1.call-start
  6.5 0.9 copy.46
  7.4 0.1 eq.42
  7.5 0.1 eq.38
  7.6 0.8 copy.52
  8.3 0.1 copy.48
  8.5 0.2 fusion.8
  8.7 0.1 add_add_fusion
  8.8 0.0 copy-start.2
  8.8 0.2 fusion.7
  9.1 0.1 reduce_sum.30
  9.2 0.1 copy.50
  9.2 0.7 multiply_add_fusion
  9.9 0.1 copy.51
  10.0 1.6 select_reduce_fusion
  11.6 1.0 convolution_convert_fusion.1
  12.7 0.1 reshape.52
  12.8 47.3 %all_to_all.10 = bf16[64,12,256]{2,1,0:T(8,128)(2,1)S(1)} all-to-all(bf16[64,12,256]{2,1,0:T(8,128)(2,1)S(1)} %reshape.52), channel_id=1, replica_groups=mesh['dp'=8,'expert'=64] {'expert'}, dimensions={0} | all-to-all | bytes 786432 | tf_op jit(solution)/shard_map/all_to_all | solution.py:36
  60.0 0.1 copy.53
  60.2 0.0 copy-start.1
  60.2 0.4 copy.54
  60.6 0.8 copy.55
  61.4 0.0 all-gather.2.cloned.1.call-update
  61.4 0.0 reduce-scatter.2.cloned.1.call-start
  61.4 30.1 %all-gather.2.cloned.1.call-done = bf16[8,2,384,256]{3,2,0,1:T(8,128)(2,1)} async-done(((bf16[1,2,384,256]{3,2,0,1:T(8,128)(2,1)}), bf16[8,2,384,256]{3,2,0,1:T(8,128)(2,1)}) %all-gather.2.cloned.1.call-update) | async-done | bytes 3145744 | tf_op jit(solution)/shard_map/all_gather | solution.py:39
  91.5 0.0 copy-done.2
  91.5 2.9 %convolution_bitcast_fusion.1 = f32[2,384,128]{2,1,0:T(8,128)S(1)} fusion(bf16[8,2,384,256]{3,2,0,1:T(8,128)(2,1)} %all-gather.2.cloned.1.call-done, bf16[2,8,256,128]{3,2,1,0:T(8,128)(2,1)S(1)} %bitcast.44), kind=kOutput, calls=%fused_computation.6 | convolution fusion | flops 402653184 | bytes 4587520 | tf_op jit(solution)/shard_map/grnd,rgdf->rnf/dot_general | solution.py:42
  94.4 0.0 copy-done
  94.4 0.0 copy-done.1
  94.4 5.4 %convolution_convert_fusion = bf16[2,384,2048]{2,1,0:T(8,128)(2,1)} fusion(bf16[2,128,2048]{2,1,0:T(8,128)(2,1)S(1)} %copy-done.1, bf16[8,2,384,256]{3,2,0,1:T(8,128)(2,1)} %all-gather.2.cloned.1.call-done, bf16[2,8,256,128]{3,2,1,0:T(8,128)(2,1)S(1)} %bitcast.38, f32[2,384,128]{2,1,0:T(8,128)S(1)} %convolution_bitcast_fusion.1), kind=kOutput, calls=%fused_computation | convolution fusion | flops 807469056 | bytes 8781824 | tf_op jit(solution)/shard_map/rnf,rfd->rnd/dot_general | solution.py:45
  99.8 0.0 reduce-scatter.2.cloned.1.call-update
  99.8 0.0 copy-start.3
  99.9 42.7 %reduce-scatter.2.cloned.1.call-done = bf16[768,256]{1,0:T(8,128)(2,1)} async-done(((bf16[768,2048]{1,0:T(8,128)(2,1)}), bf16[768,256]{1,0:T(8,128)(2,1)}) %reduce-scatter.2.cloned.1.call-update) | async-done | bytes 393232 | tf_op jit(solution)/shard_map/reduce_scatter | solution.py:47
  142.5 1.1 reshape.57
  143.7 0.1 copy.56
  143.7 0.2 copy.57
  144.0 47.1 %all_to_all.11 = bf16[64,12,256]{2,1,0:T(8,128)(2,1)S(1)} all-to-all(bf16[64,12,256]{2,1,0:T(8,128)(2,1)S(1)} %copy.57), channel_id=1, replica_groups=mesh['dp'=8,'expert'=64] {'expert'}, dimensions={0} | all-to-all | bytes 786432 | tf_op jit(solution)/shard_map/all_to_all | solution.py:50
  191.0 0.1 reshape.59
  191.1 0.0 copy-done.3
  191.1 0.8 convolution_convert_fusion.2
  (4 shorter events, 0.1 us)
Async XLA Ops:
  6.5 87.8 %copy-start = (bf16[2,2048,128]{2,1,0:T(8,128)(2,1)S(1)}, bf16[2,2048,128]{2,1,0:T(8,128)(2,1)}, u32[]{:S(2)}) copy-start(bf16[2,2048,128]{2,1,0:T(8,128)(2,1)} %param.10) | copy-start | bytes 3145732
  6.5 85.0 %all-gather.2.cloned.1.call-start = ((), (), s32[]{:S(2)}) async-start(), calls=%async_computation.3 | async-start | bytes 3538944 | tf_op jit(solution)/shard_map/all_gather | solution.py:39
  8.8 82.7 %copy-start.2 = (bf16[2,2048,128]{2,1,0:T(8,128)(2,1)S(1)}, bf16[2,2048,128]{2,1,0:T(8,128)(2,1)}, u32[]{:S(2)}) copy-start(bf16[2,2048,128]{2,1,0:T(8,128)(2,1)} %param.9) | copy-start | bytes 3145732
  60.2 34.2 %copy-start.1 = (bf16[2,128,2048]{2,1,0:T(8,128)(2,1)S(1)}, bf16[2,128,2048]{2,1,0:T(8,128)(2,1)}, u32[]{:S(2)}) copy-start(bf16[2,128,2048]{2,1,0:T(8,128)(2,1)} %param.11) | copy-start | bytes 3145732
  61.4 81.1 %reduce-scatter.2.cloned.1.call-start = ((), (), s32[]{:S(2)}) async-start(), calls=%async_computation.4 | async-start | bytes 3538944 | tf_op jit(solution)/shard_map/reduce_scatter | solution.py:47
  99.8 91.3 %copy-start.3 = (bf16[768,64]{0,1:T(8,128)(2,1)S(1)}, bf16[768,64]{0,1:T(8,128)(2,1)}, u32[]{:S(2)}) copy-start(bf16[768,64]{0,1:T(8,128)(2,1)} %get-tuple-element.5) | copy-start | bytes 294916
Sparse Core Ops, SparseCore 0:
  61.5 29.9 all-gather.1
  100.0 42.5 reduce-scatter.1

commit v2 on v0

v2 whole, which is shorter than its diff:
```python
import functools

import jax
import jax.numpy as jnp
from jax import lax
from jax.experimental import pallas as pl
from jax.experimental.pallas import tpu as pltpu
from jax.sharding import PartitionSpec as P

MESH = pl.DeviceIdType.MESH
NX, NY, NZ = 4, 4, 16
CAP = 6
SLOT = NX * 2 * CAP
GROUPS = 4
PER = NZ // GROUPS
GROWS = PER * SLOT
HALF = GROWS // 2


def kernel(
    tok_ref, ids_ref, rw_ref, wg_ref, wu_ref, wd_ref, out_ref,
    tx, meta, send, gath, wgu, wdn, comb, psib, own, sib, uni, hl, hr, fl, fr, fin, ret, acc, xout, xin,
    x_ss, x_rs, m_ss, m_rs, z_ss, z_rs, ag_ss, ag_rs, rs_ss, rs_rs, zr_ss, zr_rs, xr_ss, xr_rs, w_sem,
):
    f32, bf16 = jnp.float32, jnp.bfloat16
    rows_n, feats = tok_ref.shape
    d, ex = lax.axis_index("dp"), lax.axis_index("expert")
    y, c = d // 2, d % 2
    x, z = ex // NZ, ex % NZ
    yr, yl, yo = (y + 1) % NY, (y + NY - 1) % NY, (y + 2) % NY
    right, left, sibling = (yr * 2 + c, ex), (yl * 2 + c, ex), (y * 2 + 1 - c, ex)

    def xpeer(i):
        return (d, ((x + i) % NX) * NZ + z)

    def zpeer(o):
        return (d, x * NZ + (z + o) % NZ)

    def offset(s):
        return (s + 1) // 2 if s % 2 else (NZ - s // 2) % NZ

    def remote(src, dst, ss, rs, dev):
        return pltpu.make_async_remote_copy(
            src_ref=src, dst_ref=dst, send_sem=ss, recv_sem=rs, device_id=dev, device_id_type=MESH
        )

    sent = []

    def go(src, dst, ss, rs, dev):
        copy = remote(src, dst, ss, rs, dev)
        copy.start()
        sent.append(copy)

    def arrive(dst, ss, rs, dev):
        remote(dst, dst, ss, rs, dev).wait_recv()

    barrier = pltpu.get_barrier_semaphore()
    partners = [xpeer(i) for i in range(1, NX)] + [zpeer(o) for o in range(1, NZ)] + [right, left, sibling]
    for dev in partners:
        pl.semaphore_signal(barrier, inc=1, device_id=dev, device_id_type=MESH)

    weights = [
        pltpu.make_async_copy(wg_ref.at[0], wgu.at[:, 0:128], w_sem.at[0]),
        pltpu.make_async_copy(wg_ref.at[1], wgu.at[:, 128:256], w_sem.at[1]),
        pltpu.make_async_copy(wu_ref.at[0], wgu.at[:, 256:384], w_sem.at[2]),
        pltpu.make_async_copy(wu_ref.at[1], wgu.at[:, 384:512], w_sem.at[3]),
        pltpu.make_async_copy(wd_ref.at[0], wdn.at[0:128, :], w_sem.at[4]),
        pltpu.make_async_copy(wd_ref.at[1], wdn.at[128:256, :], w_sem.at[5]),
    ]
    for copy in weights:
        copy.start()

    meta[x] = jnp.zeros((16, 128), f32)
    meta[x, 0:8, 0:64] = ids_ref[...].astype(f32)
    meta[x, 8:16, 0:64] = rw_ref[...].astype(f32)
    tx[x] = tok_ref[...]
    acc[...] = jnp.zeros(acc.shape, f32)
    pl.semaphore_wait(barrier, len(partners))

    for i in range(1, NX):
        go(meta.at[x], meta.at[x], m_ss.at[i], m_rs.at[i], xpeer(i))
    for i in range(1, NX):
        go(tok_ref, tx.at[x], x_ss.at[i], x_rs.at[i], xpeer(i))

    shape = (NZ * 8, NX * rows_n)
    q = lax.broadcasted_iota(jnp.int32, shape, 0)
    t = lax.broadcasted_iota(jnp.int32, shape, 1)
    s = q >> 3
    off = jnp.where((s & 1) == 1, (s + 1) >> 1, (NZ - (s >> 1)) & (NZ - 1))
    expert = 2 * (x * NZ + ((z + off) & (NZ - 1))) + (q & 1)
    expert = jnp.where(((q >> 1) & (NX - 1)) == (t >> 6), expert, -1).astype(f32)
    t0 = lax.broadcasted_iota(jnp.int32, (NX * rows_n, NX * rows_n), 0)
    t1 = lax.broadcasted_iota(jnp.int32, (NX * rows_n, NX * rows_n), 1)
    before = jnp.where((t0 < t1) & ((t0 >> 6) == (t1 >> 6)), f32(1), f32(0)).astype(bf16)
    low = lax.broadcasted_iota(jnp.int32, (16, 128), 1) < 64

    for i in range(1, NX):
        arrive(meta.at[(x + NX - i) % NX], m_ss.at[i], m_rs.at[i], xpeer(i))
    info = jnp.concatenate(
        [jnp.where(low, meta[b], pltpu.roll(meta[b + 1], 64, 1)) for b in (0, 2)], axis=1
    )
    named = jnp.zeros(shape, f32)
    scale = jnp.zeros(shape, f32)
    for k in range(8):
        hit = info[k : k + 1, :] == expert
        named = named + jnp.where(hit, f32(1), f32(0))
        scale = scale + jnp.where(hit, info[8 + k : 9 + k, :], f32(0))
    rank = jnp.dot(named.astype(bf16), before, preferred_element_type=f32)
    rank = jnp.where(named > 0, rank, f32(-1)).reshape(NZ, 1, 8, NX * rows_n)
    place = lax.broadcasted_iota(jnp.int32, (NZ, CAP, 8, NX * rows_n), 1).astype(f32)
    chosen = jnp.broadcast_to(rank, place.shape) == place
    pick = jnp.where(chosen, f32(1), f32(0)).reshape(NZ * SLOT, NX * rows_n).astype(bf16)
    for i in range(1, NX):
        arrive(tx.at[(x + NX - i) % NX], x_ss.at[i], x_rs.at[i], xpeer(i))
    rows = jnp.dot(pick, tx[...].reshape(NX * rows_n, feats), preferred_element_type=f32).astype(bf16)
    send[...] = rows
    for s in range(1, NZ):
        part = pl.ds(s * SLOT, SLOT)
        go(send.at[part, :], gath.at[d, part, :], z_ss.at[s], z_rs.at[s], zpeer(offset(s)))
    gath[d, 0:SLOT, :] = rows[0:SLOT, :]
    scale = jnp.broadcast_to(scale.reshape(NZ, 1, 8, NX * rows_n), place.shape)
    mix = jnp.where(chosen, scale, f32(0)).reshape(NZ * SLOT, NX * rows_n)
    comb[...] = mix.astype(bf16)

    def group(g):
        return pl.ds(g * GROWS, GROWS)

    def first(g):
        return pl.ds(g * GROWS, HALF)

    def second(g):
        return pl.ds(g * GROWS + HALF, HALF)

    def step_own(g):
        for s in range(max(1, g * PER), (g + 1) * PER):
            arrive(gath.at[d, pl.ds(s * SLOT, SLOT), :], z_ss.at[s], z_rs.at[s], zpeer(offset(s)))
        mine = gath.at[d, group(g), :]
        go(mine, mine, ag_ss.at[g, 0], ag_rs.at[g, 0], right)
        go(mine, mine, ag_ss.at[g, 1], ag_rs.at[g, 1], left)
        go(mine, mine, ag_ss.at[g, 2], ag_rs.at[g, 2], sibling)

    def step_forward(g):
        from_l, from_r = yl * 2 + c, yr * 2 + c
        arrive(gath.at[from_l, group(g), :], ag_ss.at[g, 0], ag_rs.at[g, 0], right)
        part = gath.at[from_l, first(g), :]
        go(part, part, ag_ss.at[g, 3], ag_rs.at[g, 3], right)
        arrive(gath.at[from_r, group(g), :], ag_ss.at[g, 1], ag_rs.at[g, 1], left)
        part = gath.at[from_r, second(g), :]
        go(part, part, ag_ss.at[g, 4], ag_rs.at[g, 4], left)
        part = gath.at[from_l, group(g), :]
        go(part, part, ag_ss.at[g, 5], ag_rs.at[g, 5], sibling)
        part = gath.at[from_r, group(g), :]
        go(part, part, ag_ss.at[g, 6], ag_rs.at[g, 6], sibling)

    def step_last(g):
        far = yo * 2 + c
        arrive(gath.at[far, first(g), :], ag_ss.at[g, 3], ag_rs.at[g, 3], right)
        arrive(gath.at[far, second(g), :], ag_ss.at[g, 4], ag_rs.at[g, 4], left)
        part = gath.at[far, group(g), :]
        go(part, part, ag_ss.at[g, 7], ag_rs.at[g, 7], sibling)

    def step_experts(g):
        for i, yy in ((2, y), (5, yl), (6, yr), (7, yo)):
            arrive(gath.at[yy * 2 + 1 - c, group(g), :], ag_ss.at[g, i], ag_rs.at[g, i], sibling)
        if g == 0:
            for copy in weights:
                copy.wait()
        lhs = jnp.concatenate([gath[i, group(g), :] for i in range(2 * NY)], axis=1)
        both = jnp.dot(lhs, wgu[...], preferred_element_type=f32)
        gate, up = both[:, 0:256], both[:, 256:512]
        hidden = gate / (f32(1) + jnp.exp(-gate)) * up
        r = lax.broadcasted_iota(jnp.int32, hidden.shape, 0)
        lane = lax.broadcasted_iota(jnp.int32, hidden.shape, 1)
        hidden = jnp.where((r & 1) == (lane >> 7), hidden, f32(0)).astype(bf16)
        for yy in range(NY):
            cols = pl.ds(pl.multiple_of((2 * yy + 1 - c) * feats, feats), feats)
            psib[yy, group(g), :] = jnp.dot(hidden, wdn[:, cols], preferred_element_type=f32).astype(bf16)
        go(psib.at[:, group(g), :], sib.at[:, group(g), :], rs_ss.at[g, 0], rs_rs.at[g, 0], sibling)
        for yy in range(NY):
            cols = pl.ds(pl.multiple_of((2 * yy + c) * feats, feats), feats)
            own[yy, group(g), :] = jnp.dot(hidden, wdn[:, cols], preferred_element_type=f32)

    def step_pair(g):
        arrive(sib.at[:, group(g), :], rs_ss.at[g, 0], rs_rs.at[g, 0], sibling)
        for yy in range(NY):
            total = own[yy, group(g), :] + sib[yy, group(g), :].astype(f32)
            uni[yy, group(g), :] = total.astype(bf16)
        into = pl.ds(g * HALF, HALF)
        go(uni.at[yo, first(g), :], hl.at[into, :], rs_ss.at[g, 1], rs_rs.at[g, 1], right)
        go(uni.at[yo, second(g), :], hr.at[into, :], rs_ss.at[g, 2], rs_rs.at[g, 2], left)

    def step_near(g):
        into = pl.ds(g * HALF, HALF)
        arrive(hl.at[into, :], rs_ss.at[g, 1], rs_rs.at[g, 1], right)
        total = uni[yr, first(g), :].astype(f32) + hl[into, :].astype(f32)
        uni[yr, first(g), :] = total.astype(bf16)
        go(uni.at[yr, group(g), :], fl.at[group(g), :], rs_ss.at[g, 3], rs_rs.at[g, 3], right)
        arrive(hr.at[into, :], rs_ss.at[g, 2], rs_rs.at[g, 2], left)
        total = uni[yl, second(g), :].astype(f32) + hr[into, :].astype(f32)
        uni[yl, second(g), :] = total.astype(bf16)
        go(uni.at[yl, group(g), :], fr.at[group(g), :], rs_ss.at[g, 4], rs_rs.at[g, 4], left)

    def step_back(g):
        arrive(fl.at[group(g), :], rs_ss.at[g, 3], rs_rs.at[g, 3], right)
        arrive(fr.at[group(g), :], rs_ss.at[g, 4], rs_rs.at[g, 4], left)
        total = uni[y, group(g), :].astype(f32) + fl[group(g), :].astype(f32) + fr[group(g), :].astype(f32)
        total = total.astype(bf16)
        fin[group(g), :] = total
        for s in range(max(1, g * PER), (g + 1) * PER):
            part = pl.ds(s * SLOT, SLOT)
            go(fin.at[part, :], ret.at[part, :], zr_ss.at[s], zr_rs.at[s], zpeer(NZ - offset(s)))
        if g == 0:
            ret[0:SLOT, :] = total[0:SLOT, :]

    def step_mix(g):
        for s in range(max(1, g * PER), (g + 1) * PER):
            part = pl.ds(s * SLOT, SLOT)
            arrive(ret.at[part, :], zr_ss.at[s], zr_rs.at[s], zpeer(NZ - offset(s)))
        acc[...] += lax.dot_general(
            comb[group(g), :], ret[group(g), :], (((0,), (0,)), ((), ())), preferred_element_type=f32
        )

    steps = [step_own, step_forward, step_last, step_experts, step_pair, step_near, step_back, step_mix]
    for tick in range(GROUPS + len(steps) - 1):
        for k in reversed(range(len(steps))):
            if 0 <= tick - k < GROUPS:
                steps[k](tick - k)

    xout[...] = acc[...].astype(bf16).reshape(NX, rows_n, feats)
    for i in range(1, NX):
        go(xout.at[(x + i) % NX], xin.at[i], xr_ss.at[i], xr_rs.at[i], xpeer(i))
    total = acc[pl.ds(pl.multiple_of(x * rows_n, rows_n), rows_n), :]
    for i in range(1, NX):
        arrive(xin.at[i], xr_ss.at[i], xr_rs.at[i], xpeer(i))
        total = total + xin[i].astype(f32)
    out_ref[...] = total.astype(bf16)
    for copy in sent:
        copy.wait_send()


def on_device(tokens, expert_ids, route_weights, w_gate, w_up, w_down):
    rows_n, feats = tokens.shape
    vm, dma = pltpu.VMEM, pltpu.SemaphoreType.DMA
    bf16, f32 = jnp.bfloat16, jnp.float32
    total = NZ * SLOT
    width = w_gate.shape[1]
    in_vmem = pl.BlockSpec(memory_space=pltpu.VMEM)
    in_any = pl.BlockSpec(memory_space=pl.ANY)
    return pl.pallas_call(
        kernel,
        out_shape=jax.ShapeDtypeStruct((rows_n, feats), bf16),
        in_specs=[in_vmem] * 3 + [in_any] * 3,
        out_specs=in_vmem,
        scratch_shapes=[
            vm((NX, rows_n, feats), bf16),
            vm((NX, 16, 128), f32),
            vm((total, feats), bf16),
            vm((2 * NY, total, feats), bf16),
            vm((width, 512), bf16),
            vm((256, width), bf16),
            vm((total, NX * rows_n), bf16),
            vm((NY, total, feats), bf16),
            vm((NY, total, feats), f32),
            vm((NY, total, feats), bf16),
            vm((NY, total, feats), bf16),
            vm((total // 2, feats), bf16),
            vm((total // 2, feats), bf16),
            vm((total, feats), bf16),
            vm((total, feats), bf16),
            vm((total, feats), bf16),
            vm((total, feats), bf16),
            vm((NX * rows_n, feats), f32),
            vm((NX, rows_n, feats), bf16),
            vm((NX, rows_n, feats), bf16),
            dma((NX,)), dma((NX,)), dma((NX,)), dma((NX,)),
            dma((NZ,)), dma((NZ,)),
            dma((GROUPS, 8)), dma((GROUPS, 8)),
            dma((GROUPS, 5)), dma((GROUPS, 5)),
            dma((NZ,)), dma((NZ,)),
            dma((NX,)), dma((NX,)),
            dma((6,)),
        ],
        compiler_params=pltpu.CompilerParams(
            collective_id=0, has_side_effects=True, vmem_limit_bytes=40 << 20
        ),
    )(tokens, expert_ids.T, route_weights.T, w_gate, w_up, w_down)


def solution(mesh):
    return jax.shard_map(
        on_device,
        mesh=mesh,
        in_specs=(
            P("expert", "dp"),
            P("expert", None),
            P("expert", None),
            P("expert", None, "dp"),
            P("expert", None, "dp"),
            P("expert", "dp", None),
        ),
        out_specs=P("expert", "dp"),
        check_vma=False,
    )
```

time: 418 us -> 99.8 us (0.24)
  the two profiles are of different devices: /device:TPU:1 before, /device:TPU:16 now
where the time goes in v2:
time: 99.8 us; the launch traced here: 99.5 us
  Pallas kernels  93.1 us (93%)
  local copies, waits for them, and re-layouts  6.41 us (6%)
    pallas_call x1, Pallas kernels, on_device(): pl.pallas_call(kernel, out_shape=jax.ShapeDtypeStruct((rows_n, feats), bf...  93.1 us
    unnamed x13, local copies, waits for them, and re-layouts  6.41 us

profile of v2, /device:TPU:16, one launch (start us, length us, event | category | flops | bytes accessed | tf_op | source)
XLA Modules:
  0.0 99.5 jit_solution(2312550446254764923)
XLA Ops:
  0.0 0.0 copy-start.5
  0.0 0.7 copy-done.5
  0.7 0.0 copy-start
  0.7 1.2 %copy-done = bf16[2,2048,128]{2,1,0:T(8,128)(2,1)S(1)} copy-done((bf16[2,2048,128]{2,1,0:T(8,128)(2,1)S(1)}, bf16[2,2048,128]{2,1,0:T(8,128)(2,1)}, u32[]{:S(2)}) %copy-start) | copy-done | bytes 1048600
  1.9 0.0 copy-start.1
  1.9 1.2 %copy-done.1 = bf16[2,2048,128]{2,1,0:T(8,128)(2,1)S(1)} copy-done((bf16[2,2048,128]{2,1,0:T(8,128)(2,1)S(1)}, bf16[2,2048,128]{2,1,0:T(8,128)(2,1)}, u32[]{:S(2)}) %copy-start.1) | copy-done | bytes 1048600
  3.1 0.0 copy-start.2
  3.1 1.2 %copy-done.2 = bf16[2,128,2048]{2,1,0:T(8,128)(2,1)S(1)} copy-done((bf16[2,128,2048]{2,1,0:T(8,128)(2,1)S(1)}, bf16[2,128,2048]{2,1,0:T(8,128)(2,1)}, u32[]{:S(2)}) %copy-start.2) | copy-done | bytes 1048600
  4.4 0.0 copy-start.3
  4.4 0.8 copy-done.3
  5.1 0.0 copy-start.4
  5.1 0.7 copy-done.4
  5.8 93.1 %shard_map.64 = bf16[64,256]{1,0:T(8,128)(2,1)S(1)} custom-call(bf16[64,256]{1,0:T(8,128)(2,1)S(1)} %copy-done.3, s32[8,64]{1,0:T(8,128)S(1)} %bitcast.2, bf16[8,64]{1,0:T(8,128)(2,1)S(1)} %bitcast.3, bf16[2,2048,128]{2,1,0:T(8,128)(2,1)S(1)} %copy-done, bf16[2,2048,128]{2,1,0:T(8,128)(2,1)S(1)} %copy-done.1, bf16[2,128,2048]{2,1,0:T(8,128)(2,1)S(1)} %copy-done.2), custom_call_target="tpu_custom_call" | custom-call | tf_op jit(solution)/shard_map/pallas_call | solution.py:249
  98.9 0.6 copy.8
Async XLA Ops:
  0.0 0.7 copy-start.5
  0.7 1.2 %copy-start = (bf16[2,2048,128]{2,1,0:T(8,128)(2,1)S(1)}, bf16[2,2048,128]{2,1,0:T(8,128)(2,1)}, u32[]{:S(2)}) copy-start(bf16[2,2048,128]{2,1,0:T(8,128)(2,1)} %wg_ref.1) | copy-start | bytes 3145732
  1.9 1.2 %copy-start.1 = (bf16[2,2048,128]{2,1,0:T(8,128)(2,1)S(1)}, bf16[2,2048,128]{2,1,0:T(8,128)(2,1)}, u32[]{:S(2)}) copy-start(bf16[2,2048,128]{2,1,0:T(8,128)(2,1)} %wu_ref.1) | copy-start | bytes 3145732
  3.1 1.2 %copy-start.2 = (bf16[2,128,2048]{2,1,0:T(8,128)(2,1)S(1)}, bf16[2,128,2048]{2,1,0:T(8,128)(2,1)}, u32[]{:S(2)}) copy-start(bf16[2,128,2048]{2,1,0:T(8,128)(2,1)} %wd_ref.1) | copy-start | bytes 3145732
  4.4 0.8 copy-start.3
  5.1 0.7 copy-start.4

commit v3 on v2

--- a/solution.py
+++ b/solution.py
@@ -15,11 +15,19 @@
 PER = NZ // GROUPS
 GROWS = PER * SLOT
 HALF = GROWS // 2
+OFFSETS = (0, 8, 4, 12, 1, 9, 5, 13, 2, 10, 6, 14, 3, 11, 7, 15)
+AHEAD = 2
+ORDER = (
+    (0, 0), (1, 0), (0, 1), (2, 0), (3, 0), (0, 2), (1, 1), (4, 0),
+    (1, 2), (0, 3), (2, 1), (5, 0), (3, 1), (2, 2), (4, 1), (1, 3),
+    (3, 2), (6, 0), (5, 1), (4, 2), (2, 3), (3, 3), (6, 1), (5, 2),
+    (4, 3), (6, 2), (5, 3), (6, 3), (7, 0), (7, 1), (7, 2), (7, 3),
+)
 
 
 def kernel(
     tok_ref, ids_ref, rw_ref, wg_ref, wu_ref, wd_ref, out_ref,
-    tx, meta, send, gath, wgu, wdn, comb, psib, own, sib, uni, hl, hr, fl, fr, fin, ret, acc, xout, xin,
+    tx, ids_v, rw_v, meta, send, gath, wgu, wdn, comb, psib, own, sib, uni, hl, hr, fl, fr, fin, ret, acc, xout, xin,
     x_ss, x_rs, m_ss, m_rs, z_ss, z_rs, ag_ss, ag_rs, rs_ss, rs_rs, zr_ss, zr_rs, xr_ss, xr_rs, w_sem,
 ):
     f32, bf16 = jnp.float32, jnp.bfloat16
@@ -37,7 +45,7 @@
         return (d, x * NZ + (z + o) % NZ)
 
     def offset(s):
-        return (s + 1) // 2 if s % 2 else (NZ - s // 2) % NZ
+        return OFFSETS[s]
 
     def remote(src, dst, ss, rs, dev):
         return pltpu.make_async_remote_copy(
@@ -59,6 +67,13 @@
     for dev in partners:
         pl.semaphore_signal(barrier, inc=1, device_id=dev, device_id_type=MESH)
 
+    x_in = [
+        pltpu.make_async_copy(ids_ref, ids_v, w_sem.at[6]),
+        pltpu.make_async_copy(rw_ref, rw_v, w_sem.at[7]),
+        pltpu.make_async_copy(tok_ref, tx.at[x], w_sem.at[8]),
+    ]
+    for copy in x_in:
+        copy.start()
     weights = [
         pltpu.make_async_copy(wg_ref.at[0], wgu.at[:, 0:128], w_sem.at[0]),
         pltpu.make_async_copy(wg_ref.at[1], wgu.at[:, 128:256], w_sem.at[1]),
@@ -71,22 +86,23 @@
         copy.start()
 
     meta[x] = jnp.zeros((16, 128), f32)
-    meta[x, 0:8, 0:64] = ids_ref[...].astype(f32)
-    meta[x, 8:16, 0:64] = rw_ref[...].astype(f32)
-    tx[x] = tok_ref[...]
     acc[...] = jnp.zeros(acc.shape, f32)
+    for copy in x_in:
+        copy.wait()
+    meta[x, 0:8, 0:64] = ids_v[...].astype(f32)
+    meta[x, 8:16, 0:64] = rw_v[...].astype(f32)
     pl.semaphore_wait(barrier, len(partners))
 
     for i in range(1, NX):
         go(meta.at[x], meta.at[x], m_ss.at[i], m_rs.at[i], xpeer(i))
     for i in range(1, NX):
-        go(tok_ref, tx.at[x], x_ss.at[i], x_rs.at[i], xpeer(i))
+        go(tx.at[x], tx.at[x], x_ss.at[i], x_rs.at[i], xpeer(i))
 
     shape = (NZ * 8, NX * rows_n)
     q = lax.broadcasted_iota(jnp.int32, shape, 0)
     t = lax.broadcasted_iota(jnp.int32, shape, 1)
     s = q >> 3
-    off = jnp.where((s & 1) == 1, (s + 1) >> 1, (NZ - (s >> 1)) & (NZ - 1))
+    off = (s >> 2) + ((s & 2) << 1) + ((s & 1) << 3)
     expert = 2 * (x * NZ + ((z + off) & (NZ - 1))) + (q & 1)
     expert = jnp.where(((q >> 1) & (NX - 1)) == (t >> 6), expert, -1).astype(f32)
     t0 = lax.broadcasted_iota(jnp.int32, (NX * rows_n, NX * rows_n), 0)
@@ -114,9 +130,14 @@
         arrive(tx.at[(x + NX - i) % NX], x_ss.at[i], x_rs.at[i], xpeer(i))
     rows = jnp.dot(pick, tx[...].reshape(NX * rows_n, feats), preferred_element_type=f32).astype(bf16)
     send[...] = rows
-    for s in range(1, NZ):
-        part = pl.ds(s * SLOT, SLOT)
-        go(send.at[part, :], gath.at[d, part, :], z_ss.at[s], z_rs.at[s], zpeer(offset(s)))
+
+    def step_out(g):
+        for s in range(max(1, g * PER), (g + 1) * PER):
+            part = pl.ds(s * SLOT, SLOT)
+            go(send.at[part, :], gath.at[d, part, :], z_ss.at[s], z_rs.at[s], zpeer(offset(s)))
+
+    for g in range(AHEAD):
+        step_out(g)
     gath[d, 0:SLOT, :] = rows[0:SLOT, :]
     scale = jnp.broadcast_to(scale.reshape(NZ, 1, 8, NX * rows_n), place.shape)
     mix = jnp.where(chosen, scale, f32(0)).reshape(NZ * SLOT, NX * rows_n)
@@ -134,6 +155,8 @@
     def step_own(g):
         for s in range(max(1, g * PER), (g + 1) * PER):
             arrive(gath.at[d, pl.ds(s * SLOT, SLOT), :], z_ss.at[s], z_rs.at[s], zpeer(offset(s)))
+        if g + AHEAD < GROUPS:
+            step_out(g + AHEAD)
         mine = gath.at[d, group(g), :]
         go(mine, mine, ag_ss.at[g, 0], ag_rs.at[g, 0], right)
         go(mine, mine, ag_ss.at[g, 1], ag_rs.at[g, 1], left)
@@ -221,10 +244,8 @@
         )
 
     steps = [step_own, step_forward, step_last, step_experts, step_pair, step_near, step_back, step_mix]
-    for tick in range(GROUPS + len(steps) - 1):
-        for k in reversed(range(len(steps))):
-            if 0 <= tick - k < GROUPS:
-                steps[k](tick - k)
+    for k, g in ORDER:
+        steps[k](g)
 
     xout[...] = acc[...].astype(bf16).reshape(NX, rows_n, feats)
     for i in range(1, NX):
@@ -245,14 +266,16 @@
     total = NZ * SLOT
     width = w_gate.shape[1]
     in_vmem = pl.BlockSpec(memory_space=pltpu.VMEM)
-    in_any = pl.BlockSpec(memory_space=pl.ANY)
+    in_hbm = pl.BlockSpec(memory_space=pltpu.HBM)
     return pl.pallas_call(
         kernel,
         out_shape=jax.ShapeDtypeStruct((rows_n, feats), bf16),
-        in_specs=[in_vmem] * 3 + [in_any] * 3,
+        in_specs=[in_hbm] * 6,
         out_specs=in_vmem,
         scratch_shapes=[
             vm((NX, rows_n, feats), bf16),
+            vm((8, rows_n), jnp.int32),
+            vm((8, rows_n), bf16),
             vm((NX, 16, 128), f32),
             vm((total, feats), bf16),
             vm((2 * NY, total, feats), bf16),
@@ -278,10 +301,10 @@
             dma((GROUPS, 5)), dma((GROUPS, 5)),
             dma((NZ,)), dma((NZ,)),
             dma((NX,)), dma((NX,)),
-            dma((6,)),
+            dma((9,)),
         ],
         compiler_params=pltpu.CompilerParams(
-            collective_id=0, has_side_effects=True, vmem_limit_bytes=40 << 20
+            collective_id=0, has_side_effects=True, vmem_limit_bytes=60 << 20
         ),
     )(tokens, expert_ids.T, route_weights.T, w_gate, w_up, w_down)
 

time: 99.8 us -> 84.9 us (0.85)
  the two profiles are of different devices: /device:TPU:16 before, /device:TPU:44 now
where the time goes in v3:
time: 84.9 us; the launch traced here: 84.7 us
  Pallas kernels  83.3 us (98%)
  local copies, waits for them, and re-layouts  1.38 us (2%)
    pallas_call x1, Pallas kernels, on_device(): pl.pallas_call(kernel, out_shape=jax.ShapeDtypeStruct((rows_n, feats), bf...  83.3 us

profile of v3, /device:TPU:44, one launch (start us, length us, event | category | flops | bytes accessed | tf_op | source)
XLA Modules:
  0.0 84.7 jit_solution(5393136035041766145)
XLA Ops:
  0.0 83.3 %shard_map.64 = bf16[64,256]{1,0:T(8,128)(2,1)} custom-call(bf16[64,256]{1,0:T(8,128)(2,1)} %tok_ref.1, s32[8,64]{1,0:T(8,128)} %bitcast.2, bf16[8,64]{1,0:T(8,128)(2,1)} %bitcast.3, bf16[2,2048,128]{2,1,0:T(8,128)(2,1)} %wg_ref.1, bf16[2,2048,128]{2,1,0:T(8,128)(2,1)} %wu_ref.1, bf16[2,128,2048]{2,1,0:T(8,128)(2,1)} %wd_ref.1), custom_call_target="tpu_custom_call" | custom-call | tf_op jit(solution)/shard_map/pallas_call | solution.py:270
  83.3 1.4 %copy.8 = bf16[64,256]{1,0:T(8,128)(2,1)} copy(bf16[64,256]{1,0:T(8,128)(2,1)} %shard_map.64) | data formatting | bytes 65536

commit v4 on v3

--- a/solution.py
+++ b/solution.py
@@ -11,23 +11,26 @@
 NX, NY, NZ = 4, 4, 16
 CAP = 6
 SLOT = NX * 2 * CAP
-GROUPS = 4
-PER = NZ // GROUPS
-GROWS = PER * SLOT
-HALF = GROWS // 2
-OFFSETS = (0, 8, 4, 12, 1, 9, 5, 13, 2, 10, 6, 14, 3, 11, 7, 15)
-AHEAD = 2
+GROUPS = 7
+STARTS = (0, 2, 4, 6, 8, 10, 12, 16)
+OFFSETS = (6, 10, 5, 11, 0, 8, 3, 13, 4, 12, 7, 9, 2, 14, 1, 15)
+DIRECT = (True, False, False, False, False, True, False)
+OWN = 4
+AHEAD = 6
 ORDER = (
-    (0, 0), (1, 0), (0, 1), (2, 0), (3, 0), (0, 2), (1, 1), (4, 0),
-    (1, 2), (0, 3), (2, 1), (5, 0), (3, 1), (2, 2), (4, 1), (1, 3),
-    (3, 2), (6, 0), (5, 1), (4, 2), (2, 3), (3, 3), (6, 1), (5, 2),
-    (4, 3), (6, 2), (5, 3), (6, 3), (7, 0), (7, 1), (7, 2), (7, 3),
+    (0, 0), (0, 1), (1, 0), (0, 3), (2, 0), (1, 1), (0, 2), (3, 0),
+    (0, 4), (4, 0), (5, 0), (1, 3), (2, 1), (1, 2), (3, 1), (1, 4),
+    (4, 1), (0, 6), (0, 5), (2, 3), (6, 0), (2, 2), (2, 4), (3, 3),
+    (5, 1), (3, 2), (3, 4), (4, 3), (4, 2), (1, 6), (4, 4), (1, 5),
+    (2, 5), (6, 1), (5, 3), (3, 5), (5, 2), (2, 6), (4, 5), (5, 5),
+    (5, 4), (3, 6), (6, 3), (6, 2), (4, 6), (6, 5), (6, 4), (5, 6),
+    (6, 6), (7, 0), (7, 1), (7, 3), (7, 2), (7, 5), (7, 4), (7, 6),
 )
 
 
 def kernel(
     tok_ref, ids_ref, rw_ref, wg_ref, wu_ref, wd_ref, out_ref,
-    tx, ids_v, rw_v, meta, send, gath, wgu, wdn, comb, psib, own, sib, uni, hl, hr, fl, fr, fin, ret, acc, xout, xin,
+    tx, ids_v, rw_v, meta, send, gath, wgu, wdn, comb, psib, own, sib, uni, far, fl, fr, fin, ret, acc, xout, xin,
     x_ss, x_rs, m_ss, m_rs, z_ss, z_rs, ag_ss, ag_rs, rs_ss, rs_rs, zr_ss, zr_rs, xr_ss, xr_rs, w_sem,
 ):
     f32, bf16 = jnp.float32, jnp.bfloat16
@@ -36,7 +39,8 @@
     y, c = d // 2, d % 2
     x, z = ex // NZ, ex % NZ
     yr, yl, yo = (y + 1) % NY, (y + NY - 1) % NY, (y + 2) % NY
-    right, left, sibling = (yr * 2 + c, ex), (yl * 2 + c, ex), (y * 2 + 1 - c, ex)
+    right, left, across = (yr * 2 + c, ex), (yl * 2 + c, ex), (yo * 2 + c, ex)
+    sibling = (y * 2 + 1 - c, ex)
 
     def xpeer(i):
         return (d, ((x + i) % NX) * NZ + z)
@@ -52,7 +56,7 @@
             src_ref=src, dst_ref=dst, send_sem=ss, recv_sem=rs, device_id=dev, device_id_type=MESH
         )
 
-    sent = []
+    sent, ready = [], []
 
     def go(src, dst, ss, rs, dev):
         copy = remote(src, dst, ss, rs, dev)
@@ -62,8 +66,11 @@
     def arrive(dst, ss, rs, dev):
         remote(dst, dst, ss, rs, dev).wait_recv()
 
+    def group(g):
+        return pl.ds(STARTS[g] * SLOT, (STARTS[g + 1] - STARTS[g]) * SLOT)
+
     barrier = pltpu.get_barrier_semaphore()
-    partners = [xpeer(i) for i in range(1, NX)] + [zpeer(o) for o in range(1, NZ)] + [right, left, sibling]
+    partners = [xpeer(i) for i in range(1, NX)] + [zpeer(o) for o in range(1, NZ)] + [right, left, across, sibling]
     for dev in partners:
         pl.semaphore_signal(barrier, inc=1, device_id=dev, device_id_type=MESH)
 
@@ -102,7 +109,9 @@
     q = lax.broadcasted_iota(jnp.int32, shape, 0)
     t = lax.broadcasted_iota(jnp.int32, shape, 1)
     s = q >> 3
-    off = (s >> 2) + ((s & 2) << 1) + ((s & 1) << 3)
+    off = jnp.zeros(shape, jnp.int32)
+    for i in range(NZ):
+        off = jnp.where(s == i, OFFSETS[i], off)
     expert = 2 * (x * NZ + ((z + off) & (NZ - 1))) + (q & 1)
     expert = jnp.where(((q >> 1) & (NX - 1)) == (t >> 6), expert, -1).astype(f32)
     t0 = lax.broadcasted_iota(jnp.int32, (NX * rows_n, NX * rows_n), 0)
@@ -123,69 +132,84 @@
         scale = scale + jnp.where(hit, info[8 + k : 9 + k, :], f32(0))
     rank = jnp.dot(named.astype(bf16), before, preferred_element_type=f32)
     rank = jnp.where(named > 0, rank, f32(-1)).reshape(NZ, 1, 8, NX * rows_n)
-    place = lax.broadcasted_iota(jnp.int32, (NZ, CAP, 8, NX * rows_n), 1).astype(f32)
-    chosen = jnp.broadcast_to(rank, place.shape) == place
-    pick = jnp.where(chosen, f32(1), f32(0)).reshape(NZ * SLOT, NX * rows_n).astype(bf16)
+
+    def chosen(first, last):
+        shape = (last - first, CAP, 8, NX * rows_n)
+        place = lax.broadcasted_iota(jnp.int32, shape, 1).astype(f32)
+        return jnp.broadcast_to(rank[first:last], shape) == place
+
     for i in range(1, NX):
         arrive(tx.at[(x + NX - i) % NX], x_ss.at[i], x_rs.at[i], xpeer(i))
-    rows = jnp.dot(pick, tx[...].reshape(NX * rows_n, feats), preferred_element_type=f32).astype(bf16)
-    send[...] = rows
+    block = tx[...].reshape(NX * rows_n, feats)
 
     def step_out(g):
-        for s in range(max(1, g * PER), (g + 1) * PER):
+        pick = jnp.where(chosen(STARTS[g], STARTS[g + 1]), f32(1), f32(0))
+        pick = pick.reshape((STARTS[g + 1] - STARTS[g]) * SLOT, NX * rows_n).astype(bf16)
+        send[group(g), :] = jnp.dot(pick, block, preferred_element_type=f32).astype(bf16)
+        for s in range(STARTS[g], STARTS[g + 1]):
             part = pl.ds(s * SLOT, SLOT)
-            go(send.at[part, :], gath.at[d, part, :], z_ss.at[s], z_rs.at[s], zpeer(offset(s)))
+            if s == OWN:
+                gath[d, part, :] = send[part, :]
+            else:
+                go(send.at[part, :], gath.at[d, part, :], z_ss.at[s], z_rs.at[s], zpeer(offset(s)))
 
     for g in range(AHEAD):
         step_out(g)
-    gath[d, 0:SLOT, :] = rows[0:SLOT, :]
-    scale = jnp.broadcast_to(scale.reshape(NZ, 1, 8, NX * rows_n), place.shape)
-    mix = jnp.where(chosen, scale, f32(0)).reshape(NZ * SLOT, NX * rows_n)
+    scale = jnp.broadcast_to(scale.reshape(NZ, 1, 8, NX * rows_n), (NZ, CAP, 8, NX * rows_n))
+    mix = jnp.where(chosen(0, NZ), scale, f32(0)).reshape(NZ * SLOT, NX * rows_n)
     comb[...] = mix.astype(bf16)
 
-    def group(g):
-        return pl.ds(g * GROWS, GROWS)
+    def half(g):
+        return ((STARTS[g + 1] - STARTS[g]) * SLOT // 2 + 15) // 16 * 16
 
     def first(g):
-        return pl.ds(g * GROWS, HALF)
+        return pl.ds(STARTS[g] * SLOT, half(g))
 
     def second(g):
-        return pl.ds(g * GROWS + HALF, HALF)
+        return pl.ds(STARTS[g] * SLOT + half(g), (STARTS[g + 1] - STARTS[g]) * SLOT - half(g))
 
     def step_own(g):
-        for s in range(max(1, g * PER), (g + 1) * PER):
+        for s in [i for i in range(STARTS[g], STARTS[g + 1]) if i != OWN]:
             arrive(gath.at[d, pl.ds(s * SLOT, SLOT), :], z_ss.at[s], z_rs.at[s], zpeer(offset(s)))
         if g + AHEAD < GROUPS:
             step_out(g + AHEAD)
         mine = gath.at[d, group(g), :]
         go(mine, mine, ag_ss.at[g, 0], ag_rs.at[g, 0], right)
         go(mine, mine, ag_ss.at[g, 1], ag_rs.at[g, 1], left)
+        if DIRECT[g]:
+            go(mine, mine, ag_ss.at[g, 3], ag_rs.at[g, 3], across)
         go(mine, mine, ag_ss.at[g, 2], ag_rs.at[g, 2], sibling)
 
     def step_forward(g):
         from_l, from_r = yl * 2 + c, yr * 2 + c
         arrive(gath.at[from_l, group(g), :], ag_ss.at[g, 0], ag_rs.at[g, 0], right)
-        part = gath.at[from_l, first(g), :]
-        go(part, part, ag_ss.at[g, 3], ag_rs.at[g, 3], right)
+        if not DIRECT[g]:
+            part = gath.at[from_l, first(g), :]
+            go(part, part, ag_ss.at[g, 3], ag_rs.at[g, 3], right)
         arrive(gath.at[from_r, group(g), :], ag_ss.at[g, 1], ag_rs.at[g, 1], left)
-        part = gath.at[from_r, second(g), :]
-        go(part, part, ag_ss.at[g, 4], ag_rs.at[g, 4], left)
+        if not DIRECT[g]:
+            part = gath.at[from_r, second(g), :]
+            go(part, part, ag_ss.at[g, 4], ag_rs.at[g, 4], left)
         part = gath.at[from_l, group(g), :]
         go(part, part, ag_ss.at[g, 5], ag_rs.at[g, 5], sibling)
         part = gath.at[from_r, group(g), :]
         go(part, part, ag_ss.at[g, 6], ag_rs.at[g, 6], sibling)
 
     def step_last(g):
-        far = yo * 2 + c
-        arrive(gath.at[far, first(g), :], ag_ss.at[g, 3], ag_rs.at[g, 3], right)
-        arrive(gath.at[far, second(g), :], ag_ss.at[g, 4], ag_rs.at[g, 4], left)
-        part = gath.at[far, group(g), :]
+        other = yo * 2 + c
+        if DIRECT[g]:
+            arrive(gath.at[other, group(g), :], ag_ss.at[g, 3], ag_rs.at[g, 3], across)
+        else:
+            arrive(gath.at[other, first(g), :], ag_ss.at[g, 3], ag_rs.at[g, 3], right)
+            arrive(gath.at[other, second(g), :], ag_ss.at[g, 4], ag_rs.at[g, 4], left)
+        part = gath.at[other, group(g), :]
         go(part, part, ag_ss.at[g, 7], ag_rs.at[g, 7], sibling)
 
     def step_experts(g):
         for i, yy in ((2, y), (5, yl), (6, yr), (7, yo)):
             arrive(gath.at[yy * 2 + 1 - c, group(g), :], ag_ss.at[g, i], ag_rs.at[g, i], sibling)
-        if g == 0:
+        if not ready:
+            ready.append(True)
             for copy in weights:
                 copy.wait()
         lhs = jnp.concatenate([gath[i, group(g), :] for i in range(2 * NY)], axis=1)
@@ -208,18 +232,23 @@
         for yy in range(NY):
             total = own[yy, group(g), :] + sib[yy, group(g), :].astype(f32)
             uni[yy, group(g), :] = total.astype(bf16)
-        into = pl.ds(g * HALF, HALF)
-        go(uni.at[yo, first(g), :], hl.at[into, :], rs_ss.at[g, 1], rs_rs.at[g, 1], right)
-        go(uni.at[yo, second(g), :], hr.at[into, :], rs_ss.at[g, 2], rs_rs.at[g, 2], left)
+        if DIRECT[g]:
+            go(uni.at[yo, group(g), :], far.at[group(g), :], rs_ss.at[g, 1], rs_rs.at[g, 1], across)
+            go(uni.at[yr, group(g), :], fl.at[group(g), :], rs_ss.at[g, 3], rs_rs.at[g, 3], right)
+            go(uni.at[yl, group(g), :], fr.at[group(g), :], rs_ss.at[g, 4], rs_rs.at[g, 4], left)
+        else:
+            go(uni.at[yo, first(g), :], far.at[first(g), :], rs_ss.at[g, 1], rs_rs.at[g, 1], right)
+            go(uni.at[yo, second(g), :], far.at[second(g), :], rs_ss.at[g, 2], rs_rs.at[g, 2], left)
 
     def step_near(g):
-        into = pl.ds(g * HALF, HALF)
-        arrive(hl.at[into, :], rs_ss.at[g, 1], rs_rs.at[g, 1], right)
-        total = uni[yr, first(g), :].astype(f32) + hl[into, :].astype(f32)
+        if DIRECT[g]:
+            return
+        arrive(far.at[first(g), :], rs_ss.at[g, 1], rs_rs.at[g, 1], right)
+        total = uni[yr, first(g), :].astype(f32) + far[first(g), :].astype(f32)
         uni[yr, first(g), :] = total.astype(bf16)
         go(uni.at[yr, group(g), :], fl.at[group(g), :], rs_ss.at[g, 3], rs_rs.at[g, 3], right)
-        arrive(hr.at[into, :], rs_ss.at[g, 2], rs_rs.at[g, 2], left)
-        total = uni[yl, second(g), :].astype(f32) + hr[into, :].astype(f32)
+        arrive(far.at[second(g), :], rs_ss.at[g, 2], rs_rs.at[g, 2], left)
+        total = uni[yl, second(g), :].astype(f32) + far[second(g), :].astype(f32)
         uni[yl, second(g), :] = total.astype(bf16)
         go(uni.at[yl, group(g), :], fr.at[group(g), :], rs_ss.at[g, 4], rs_rs.at[g, 4], left)
 
@@ -227,16 +256,19 @@
         arrive(fl.at[group(g), :], rs_ss.at[g, 3], rs_rs.at[g, 3], right)
         arrive(fr.at[group(g), :], rs_ss.at[g, 4], rs_rs.at[g, 4], left)
         total = uni[y, group(g), :].astype(f32) + fl[group(g), :].astype(f32) + fr[group(g), :].astype(f32)
+        if DIRECT[g]:
+            arrive(far.at[group(g), :], rs_ss.at[g, 1], rs_rs.at[g, 1], across)
+            total = total + far[group(g), :].astype(f32)
         total = total.astype(bf16)
         fin[group(g), :] = total
-        for s in range(max(1, g * PER), (g + 1) * PER):
+        for s in [i for i in range(STARTS[g], STARTS[g + 1]) if i != OWN]:
             part = pl.ds(s * SLOT, SLOT)
             go(fin.at[part, :], ret.at[part, :], zr_ss.at[s], zr_rs.at[s], zpeer(NZ - offset(s)))
-        if g == 0:
-            ret[0:SLOT, :] = total[0:SLOT, :]
+        if STARTS[g] <= OWN < STARTS[g + 1]:
+            ret[OWN * SLOT : (OWN + 1) * SLOT, :] = fin[OWN * SLOT : (OWN + 1) * SLOT, :]
 
     def step_mix(g):
-        for s in range(max(1, g * PER), (g + 1) * PER):
+        for s in [i for i in range(STARTS[g], STARTS[g + 1]) if i != OWN]:
             part = pl.ds(s * SLOT, SLOT)
             arrive(ret.at[part, :], zr_ss.at[s], zr_rs.at[s], zpeer(NZ - offset(s)))
         acc[...] += lax.dot_general(
@@ -251,11 +283,13 @@
     for i in range(1, NX):
         go(xout.at[(x + i) % NX], xin.at[i], xr_ss.at[i], xr_rs.at[i], xpeer(i))
     total = acc[pl.ds(pl.multiple_of(x * rows_n, rows_n), rows_n), :]
+    for copy in sent[: 1 - NX]:
+        copy.wait_send()
     for i in range(1, NX):
         arrive(xin.at[i], xr_ss.at[i], xr_rs.at[i], xpeer(i))
         total = total + xin[i].astype(f32)
     out_ref[...] = total.astype(bf16)
-    for copy in sent:
+    for copy in sent[1 - NX :]:
         copy.wait_send()
 
 
@@ -286,8 +320,7 @@
             vm((NY, total, feats), f32),
             vm((NY, total, feats), bf16),
             vm((NY, total, feats), bf16),
-            vm((total // 2, feats), bf16),
-            vm((total // 2, feats), bf16),
+            vm((total, feats), bf16),
             vm((total, feats), bf16),
             vm((total, feats), bf16),
             vm((total, feats), bf16),

time: 84.9 us -> 80.2 us (0.945)
  the two profiles are of different devices: /device:TPU:44 before, /device:TPU:1 now
where the time goes in v4:
time: 80.2 us; the launch traced here: 79.6 us
  Pallas kernels  78.2 us (98%)
  local copies, waits for them, and re-layouts  1.38 us (2%)
    pallas_call x1, Pallas kernels, on_device(): pl.pallas_call(kernel, out_shape=jax.ShapeDtypeStruct((rows_n, feats), bf...  78.2 us

profile of v4, /device:TPU:1, one launch (start us, length us, event | category | flops | bytes accessed | tf_op | source)
XLA Modules:
  0.0 79.6 jit_solution(554168449637852662)
XLA Ops:
  0.0 78.2 %shard_map.64 = bf16[64,256]{1,0:T(8,128)(2,1)} custom-call(bf16[64,256]{1,0:T(8,128)(2,1)} %tok_ref.1, s32[8,64]{1,0:T(8,128)} %bitcast.2, bf16[8,64]{1,0:T(8,128)(2,1)} %bitcast.3, bf16[2,2048,128]{2,1,0:T(8,128)(2,1)} %wg_ref.1, bf16[2,2048,128]{2,1,0:T(8,128)(2,1)} %wu_ref.1, bf16[2,128,2048]{2,1,0:T(8,128)(2,1)} %wd_ref.1), custom_call_target="tpu_custom_call" | custom-call | tf_op jit(solution)/shard_map/pallas_call | solution.py:304
  78.2 1.4 %copy.8 = bf16[64,256]{1,0:T(8,128)(2,1)} copy(bf16[64,256]{1,0:T(8,128)(2,1)} %shard_map.64) | data formatting | bytes 65536

commit v5 on v4

--- a/solution.py
+++ b/solution.py
@@ -16,7 +16,7 @@
 OFFSETS = (6, 10, 5, 11, 0, 8, 3, 13, 4, 12, 7, 9, 2, 14, 1, 15)
 DIRECT = (True, False, False, False, False, True, False)
 OWN = 4
-AHEAD = 6
+AHEAD = 4
 ORDER = (
     (0, 0), (0, 1), (1, 0), (0, 3), (2, 0), (1, 1), (0, 2), (3, 0),
     (0, 4), (4, 0), (5, 0), (1, 3), (2, 1), (1, 2), (3, 1), (1, 4),

time: 80.2 us -> 79.3 us (0.989)
  no operation moved by 1% of the time
where the time goes in v5:
time: 79.3 us; the launch traced here: 79.1 us
  Pallas kernels  77.7 us (98%)
  local copies, waits for them, and re-layouts  1.38 us (2%)
    pallas_call x1, Pallas kernels, on_device(): pl.pallas_call(kernel, out_shape=jax.ShapeDtypeStruct((rows_n, feats), bf...  77.7 us

profile of v5, /device:TPU:1, one launch (start us, length us, event | category | flops | bytes accessed | tf_op | source)
XLA Modules:
  0.0 79.1 jit_solution(12234313032844061)
XLA Ops:
  0.0 77.7 %shard_map.64 = bf16[64,256]{1,0:T(8,128)(2,1)} custom-call(bf16[64,256]{1,0:T(8,128)(2,1)} %tok_ref.1, s32[8,64]{1,0:T(8,128)} %bitcast.2, bf16[8,64]{1,0:T(8,128)(2,1)} %bitcast.3, bf16[2,2048,128]{2,1,0:T(8,128)(2,1)} %wg_ref.1, bf16[2,2048,128]{2,1,0:T(8,128)(2,1)} %wu_ref.1, bf16[2,128,2048]{2,1,0:T(8,128)(2,1)} %wd_ref.1), custom_call_target="tpu_custom_call" | custom-call | tf_op jit(solution)/shard_map/pallas_call | solution.py:304
  77.7 1.4 %copy.8 = bf16[64,256]{1,0:T(8,128)(2,1)} copy(bf16[64,256]{1,0:T(8,128)(2,1)} %shard_map.64) | data formatting | bytes 65536
